TPU v7x, 32 devices: a whole 2x2x4 slice. The times are simulated.
32 devices in a mesh: query: 8 (over z, y), item: 4 (over x, core).
Axes of the slice: x: 2, y: 2, z: 4, core: 2. Of those that a mesh axis runs over, the one named last changes fastest.
Arguments:
- query_emb: bfloat16 [2048, 256], P(('query', 'item')), may hold values from -400 to 400
- targets: int32 [2048], P('query'), may hold values from 0 to 8191, as said below
- eligible_tiles: int32 [32, 32], P('query', 'item'), may hold values from 0 to 1, as said below
- item_feats: bfloat16 [4, 2048, 512], P('item', 'query'), may hold values from -6 to 6
- w_first: bfloat16 [512, 1024], replicated, may hold values from -0.25 to 0.25
- w_second: bfloat16 [1024, 256], replicated, may hold values from -0.1875 to 0.1875
Outputs:
- loss: float32 [2048], P(('query', 'item'))
- query_grad: float32 [2048, 256], P(('query', 'item'))
- w_first_grad: float32 [512, 1024], replicated
- w_second_grad: float32 [1024, 256], replicated
Inputs may be any that keep to these rules, and one draw needn't show every extreme that they name: `eligible_tiles`: every row has at least one 1. The block targets[q] // 256 is marked 1 in row q // 64 of eligible_tiles.
All inputs are finite; a program needn't handle non-finite values.
Results may differ from a plain program's by a relative error of at most 0.007.
Values may be sent and summed in bfloat16 or wider, within the bound.
A program may use at most 64 MiB of HBM per device.

v0:
```python
import math
import jax
import jax.numpy as jnp
from jax import lax
from jax.sharding import PartitionSpec as P

BOTH = ("query", "item")


def on_device(query_emb, targets, eligible_tiles, item_feats, w_first, w_second):
    q_rows = query_emb.shape[0]
    item_count = lax.axis_size("item")
    query_count = lax.axis_size("query")
    item_pos = lax.axis_index("item")
    query_pos = lax.axis_index("query")
    tokens = item_feats.reshape(item_feats.shape[1], item_feats.shape[2])
    block_rows = tokens.shape[0]
    queries = lax.all_gather(query_emb, "query", axis=0, tiled=True)
    own_targets = lax.dynamic_slice_in_dim(targets, item_pos * q_rows, q_rows, 0)
    small = jnp.concatenate([eligible_tiles.reshape(-1), own_targets])
    small = lax.all_gather(small, BOTH, axis=0).reshape(query_count, item_count, -1)
    flags = small[:, :, : eligible_tiles.size].reshape(
        (query_count, item_count) + eligible_tiles.shape
    )
    flags = lax.dynamic_slice(
        flags, (0, 0, item_pos, query_pos), (query_count, item_count, 1, 1)
    ).reshape(query_count, item_count)
    wanted = lax.dynamic_slice_in_dim(small[:, :, eligible_tiles.size :], item_pos, 1, 1).reshape(
        -1
    )
    pre_act = jnp.dot(tokens, w_first, preferred_element_type=jnp.float32)
    hidden = jax.nn.silu(pre_act).astype(jnp.bfloat16)
    own_emb = jnp.dot(hidden, w_second, preferred_element_type=jnp.float32).astype(jnp.bfloat16)
    items = lax.all_gather(own_emb, "item", axis=0, tiled=True)
    block_of = jnp.arange(item_count, dtype=jnp.int32) * query_count + query_pos
    item_ids = (
        block_of[:, None] * block_rows + jnp.arange(block_rows, dtype=jnp.int32)[None, :]
    ).reshape(-1)
    live = jnp.broadcast_to(
        flags[:, None, :, None] > 0, (query_count, q_rows, item_count, block_rows)
    ).reshape(query_count * q_rows, item_count * block_rows)
    scores = 0.25 * jnp.einsum("qe,ie->qi", queries, items, preferred_element_type=jnp.float32)
    hit = item_ids[None, :] == wanted[:, None]
    masked = jnp.where(live, scores, -1e30)
    top = jnp.max(masked, axis=1)
    total = jnp.sum(jnp.where(live, jnp.exp(masked - top[:, None]), 0.0), axis=1)
    positive = jnp.sum(jnp.where(hit, scores, 0.0), axis=1)
    stats = lax.all_gather(jnp.stack([top, total, positive]), "query", axis=0)
    all_top = jnp.max(stats[:, 0], axis=0)
    all_total = jnp.sum(stats[:, 1] * jnp.exp(stats[:, 0] - all_top[None]), axis=0)
    log_norm = all_top + jnp.log(all_total)
    loss = lax.dynamic_slice_in_dim(
        log_norm - jnp.sum(stats[:, 2], axis=0), query_pos * q_rows, q_rows, 0
    )
    weights = jnp.where(live, jnp.exp(masked - log_norm[:, None]), 0.0)
    coeffs = (weights - hit.astype(jnp.float32)).astype(jnp.bfloat16)
    e_part = 0.25 * jnp.einsum("qi,qe->ie", coeffs, queries, preferred_element_type=jnp.float32)
    own_grad = lax.psum_scatter(e_part, "item", scatter_dimension=0, tiled=True).astype(
        jnp.bfloat16
    )
    q_part = 0.25 * jnp.dot(coeffs, items, preferred_element_type=jnp.float32)
    query_grad = lax.psum_scatter(q_part, "query", scatter_dimension=0, tiled=True)
    second_term = jnp.einsum("ih,ie->he", hidden, own_grad, preferred_element_type=jnp.float32)
    hid_grad = jnp.einsum("ie,he->ih", own_grad, w_second, preferred_element_type=jnp.float32)
    gate_sig = jax.nn.sigmoid(pre_act)
    pre_grad = (hid_grad * gate_sig * (1.0 + pre_act * (1.0 - gate_sig))).astype(jnp.bfloat16)
    first_term = jnp.einsum("id,ih->dh", tokens, pre_grad, preferred_element_type=jnp.float32)
    tower_sums = lax.psum((first_term, second_term), BOTH)
    grad_scale = 1.0 / math.sqrt(block_rows * query_count * item_count)
    return (loss, query_grad, tower_sums[0] * grad_scale, tower_sums[1] * grad_scale)


def solution(mesh):
    return jax.shard_map(
        on_device,
        mesh=mesh,
        in_specs=(
            P(("query", "item"), None),
            P("query"),
            P("query", "item"),
            P("item", "query", None),
            P(),
            P(),
        ),
        out_specs=(P(("query", "item")), P(("query", "item"), None), P(), P()),
        check_vma=False,
    )
```

profile of v0, /device:TPU:0, one launch (start us, length us, event | category | flops | bytes accessed | tf_op | source)
XLA Modules:
  0.0 311.0 jit_solution(3521980565822129825)
XLA Ops:
  8.0 0.0 copy-start
  8.0 0.0 copy-start.2
  8.0 0.0 reduce-scatter.5.cloned.1.call-start
  8.1 0.9 reshape.62
  8.9 0.1 add_bitcast_fusion
  9.0 0.8 dynamic_slice.12
  9.8 0.2 add_dynamic-update-slice_fusion
  9.9 42.1 %all-reduce = s32[3072]{0:T(1024)S(1)} all-reduce(s32[3072]{0:T(1024)S(1)} %add_dynamic-update-slice_fusion), channel_id=2, replica_groups=mesh['query'=8,'item'=4] {'query','item'}, use_global_device_ids=true, to_apply=%add | all-reduce | flops 3072 | bytes 24576
  52.1 0.1 reshape.63
  52.1 0.1 slice.22
  52.2 0.1 eq.16
  52.3 0.1 copy.26
  52.4 0.1 copy.20
  52.5 31.0 %all_gather.21 = bf16[512,256]{1,0:T(8,128)(2,1)S(1)} all-gather(bf16[64,256]{1,0:T(8,128)(2,1)} %param.6), channel_id=1, replica_groups=mesh['query'=8,'item'=4] {'query'}, dimensions={0}, use_global_device_ids=true | all-gather | bytes 294912 | tf_op jit(solution)/shard_map/all_gather | solution.py:18
  83.5 0.3 broadcast_in_dim.19
  83.9 0.0 copy-start.3
  83.9 0.3 copy.30
  84.2 0.6 copy.21
  84.8 0.0 copy-done
  84.8 0.0 copy-done.2
  84.8 0.4 fusion.11
  85.2 0.0 copy-done.3
  85.3 0.0 copy-start.1
  85.3 0.4 convolution_convert_fusion
  85.7 0.5 copy-done.1
  86.2 8.0 %all_gather.20 = bf16[1024,256]{1,0:T(8,128)(2,1)S(1)} all-gather(bf16[256,256]{1,0:T(8,128)(2,1)S(1)} %convolution_convert_fusion), channel_id=1, replica_groups=mesh['query'=8,'item'=4] {'item'}, dimensions={0}, use_global_device_ids=true | all-gather | bytes 655360 | tf_op jit(solution)/shard_map/all_gather | solution.py:34
  94.2 0.6 fusion.3
  94.8 0.8 select_reduce_fusion
  95.7 30.5 %all-gather.2 = f32[8,3,512]{2,1,0:T(4,128)S(1)} all-gather(f32[1,3,512]{2,1,0:T(4,128)S(1)} %maximum_bitcast_fusion), channel_id=3, replica_groups=mesh['query'=8,'item'=4] {'query'}, dimensions={0}, use_global_device_ids=true | all-gather | bytes 55296 | tf_op jit(solution)/shard_map/all_gather | solution.py:48
  126.2 0.1 fusion.24
  126.3 0.8 fusion.2
  127.1 1.4 convolution_multiply_fusion.1
  128.5 0.0 reduce-scatter.5.cloned.1.call-update
  128.5 0.0 all-reduce.4.cloned.1.call-start
  128.6 23.9 %reduce-scatter.5.cloned.1.call-done = f32[256,256]{1,0:T(8,128)} async-done(((f32[1024,256]{1,0:T(8,128)}), f32[256,256]{1,0:T(8,128)}) %reduce-scatter.5.cloned.1.call-update) | async-done | bytes 262160 | tf_op jit(solution)/shard_map/reduce_scatter | solution.py:58
  152.4 2.8 fusion.13
  155.2 3.4 %convolution_bitcast_fusion = f32[512,1024]{0,1:T(8,128)} fusion(bf16[1024,256]{1,0:T(8,128)(2,1)S(1)} %copy-done.3, f32[256,1024]{1,0:T(8,128)} %copy-done.1, bf16[1,256,512]{2,1,0:T(8,128)(2,1)S(1)} %copy-done.2, f32[256,256]{1,0:T(8,128)} %reduce-scatter.5.cloned.1.call-done), kind=kOutput, calls=%fused_computation.7 | convolution fusion | flops 405078016 | bytes 4194304 | tf_op jit(solution)/shard_map/id,ih->dh/dot_general | solution.py:67
  158.7 0.0 all-reduce.4.cloned.1.call-update
  158.7 0.0 reduce-scatter.3.cloned.1.call-start
  158.8 1.3 convolution_multiply_fusion.2
  160.0 0.0 reduce-scatter.3.cloned.1.call-update
  160.1 0.6 dynamic_slice.15
  160.6 136.9 %all-reduce.4.cloned.1.call-done = (f32[512,1024]{0,1:T(8,128)}, f32[1024,256]{1,0:T(8,128)}) async-done(((f32[512,1024]{0,1:T(8,128)}, f32[1024,256]{1,0:T(8,128)}), (f32[512,1024]{0,1:T(8,128)}, f32[1024,256]{1,0:T(8,128)})) %all-reduce.4.cloned.1.call-update) | async-done | bytes 3145744 | tf_op jit(solution)/shard_map/psum | solution.py:68
  297.6 1.8 broadcast_multiply_fusion
  299.4 1.8 copy.25
  301.2 2.3 broadcast_multiply_fusion.1
  303.5 0.0 reduce-scatter.3.cloned.1.call-done
  (8 shorter events, 0.1 us)
Async XLA Ops:
  8.0 76.8 %copy-start = (bf16[512,1024]{1,0:T(8,128)(2,1)S(1)}, bf16[512,1024]{1,0:T(8,128)(2,1)}, u32[]{:S(2)}) copy-start(bf16[512,1024]{1,0:T(8,128)(2,1)} %param.10) | copy-start | bytes 3145732
  8.0 76.8 %copy-start.2 = (bf16[1,256,512]{2,1,0:T(8,128)(2,1)S(1)}, bf16[1,256,512]{2,1,0:T(8,128)(2,1)}, u32[]{:S(2)}) copy-start(bf16[1,256,512]{2,1,0:T(8,128)(2,1)} %param.9) | copy-start | bytes 786436
  8.0 144.4 %reduce-scatter.5.cloned.1.call-start = ((), (), s32[]{:S(2)}) async-start(), calls=%async_computation.3 | async-start | bytes 1310720 | tf_op jit(solution)/shard_map/reduce_scatter | solution.py:58
  83.9 1.4 copy-start.3
  85.3 1.0 copy-start.1
  128.5 169.1 %all-reduce.4.cloned.1.call-start = ((), (), s32[]{:S(2)}) async-start(), calls=%async_computation.4 | async-start | bytes 6291456 | tf_op jit(solution)/shard_map/psum | solution.py:68
  158.7 144.8 %reduce-scatter.3.cloned.1.call-start = ((), (), s32[]{:S(2)}) async-start(), calls=%async_computation.2 | async-start | bytes 589824 | tf_op jit(solution)/shard_map/reduce_scatter | solution.py:62
Sparse Core Ops, SparseCore 0:
  128.6 23.7 reduce-scatter.4
  158.8 138.7 all-reduce.3
Sparse Core Ops, SparseCore 1:
  163.1 62.8 reduce-scatter.2
where the time goes:
time: 311 us
  waiting for transfers between devices  161 us (52%)
  blocking collectives  112 us (36%)
  between operations  15.7 us (5%)
  matrix products  10.3 us (3%)
  local copies, waits for them, and re-layouts  6.23 us (2%)
  other arithmetic  6.14 us (2%)
    psum x1, waiting for transfers between devices, on_device(): tower_sums = lax.psum((first_term, second_term), BOTH)  137 us
    unnamed x1, blocking collectives  42.1 us
    all_gather x1, blocking collectives, on_device(): queries = lax.all_gather(query_emb, 'query', axis=0, tiled=True)  31 us
    all_gather x1, blocking collectives, on_device(): stats = lax.all_gather(jnp.stack([top, total, positive]), 'query', axis=0)  30.5 us
    reduce_scatter x1, waiting for transfers between devices, on_device(): lax.psum_scatter(e_part, 'item', scatter_dimension=0, tiled=True)  23.9 us
    all_gather x1, blocking collectives, on_device(): items = lax.all_gather(own_emb, 'item', axis=0, tiled=True)  8.01 us
  transfers between devices with their start and end apart: 3, of which 2 were waited for; matrix products, arithmetic and copies ran while one was open for 3% of the time, Pallas kernels for 0%

commit v1 on v0

--- a/solution.py
+++ b/solution.py
@@ -65,7 +65,8 @@
     gate_sig = jax.nn.sigmoid(pre_act)
     pre_grad = (hid_grad * gate_sig * (1.0 + pre_act * (1.0 - gate_sig))).astype(jnp.bfloat16)
     first_term = jnp.einsum("id,ih->dh", tokens, pre_grad, preferred_element_type=jnp.float32)
-    tower_sums = lax.psum((first_term, second_term), BOTH)
+    half = lax.psum((first_term, second_term), "item")
+    tower_sums = lax.psum(half, "query")
     grad_scale = 1.0 / math.sqrt(block_rows * query_count * item_count)
     return (loss, query_grad, tower_sums[0] * grad_scale, tower_sums[1] * grad_scale)
 

time: 311 us -> 432 us (1.39)
  waiting for transfers between devices: 161 us -> 283 us
    psum x1 -> x2, waiting for transfers between devices: 137 us -> 200 us  [the longest x1 132 us: on_device(): tower_sums = lax.psum(half, 'query')]
    reduce_scatter x1, waiting for transfers between devices: 0.01 us -> 58.7 us  [on_device(): lax.psum_scatter(q_part, 'query', scatter_dimension=0, tiled=True)]
  transfers between devices with their start and end apart: 3 -> 4, of which waited for: 2 -> 4; matrix products, arithmetic and copies ran while one was open for 3% -> 2% of each run, Pallas kernels for 0% -> 0%
where the time goes in v1:
time: 432 us
  waiting for transfers between devices  283 us (66%)
  blocking collectives  112 us (26%)
  between operations  13.9 us (3%)
  matrix products  10.3 us (2%)
  local copies, waits for them, and re-layouts  6.24 us (1%)
  other arithmetic  6.14 us (1%)
    psum x1, waiting for transfers between devices, on_device(): tower_sums = lax.psum(half, 'query')  132 us
    psum x1, waiting for transfers between devices, on_device(): half = lax.psum((first_term, second_term), 'item')  68.7 us
    reduce_scatter x1, waiting for transfers between devices, on_device(): lax.psum_scatter(q_part, 'query', scatter_dimension=0, tiled=True)  58.7 us
    unnamed x1, blocking collectives  42.1 us
    all_gather x1, blocking collectives, on_device(): queries = lax.all_gather(query_emb, 'query', axis=0, tiled=True)  31 us
    all_gather x1, blocking collectives, on_device(): stats = lax.all_gather(jnp.stack([top, total, positive]), 'query', axis=0)  30.5 us
    reduce_scatter x1, waiting for transfers between devices, on_device(): lax.psum_scatter(e_part, 'item', scatter_dimension=0, tiled=True)  23.9 us
  transfers between devices with their start and end apart: 4, of which 4 were waited for; matrix products, arithmetic and copies ran while one was open for 2% of the time, Pallas kernels for 0%

profile of v1, /device:TPU:0, one launch (start us, length us, event | category | flops | bytes accessed | tf_op | source)
XLA Modules:
  0.0 431.5 jit_solution(1064269458471591446)
XLA Ops:
  7.2 0.0 copy-start
  7.2 0.0 copy-start.2
  7.2 0.0 reduce-scatter.5.cloned.1.call-start
  7.3 0.9 reshape.62
  8.1 0.1 add_bitcast_fusion
  8.2 0.8 dynamic_slice.12
  8.9 0.2 add_dynamic-update-slice_fusion
  9.1 42.1 %all-reduce = s32[3072]{0:T(1024)S(1)} all-reduce(s32[3072]{0:T(1024)S(1)} %add_dynamic-update-slice_fusion), channel_id=2, replica_groups=mesh['query'=8,'item'=4] {'query','item'}, use_global_device_ids=true, to_apply=%add | all-reduce | flops 3072 | bytes 24576
  51.2 0.1 reshape.63
  51.3 0.1 slice.22
  51.4 0.1 eq.16
  51.5 0.1 copy.26
  51.6 0.1 copy.20
  51.7 31.0 %all_gather.21 = bf16[512,256]{1,0:T(8,128)(2,1)S(1)} all-gather(bf16[64,256]{1,0:T(8,128)(2,1)} %param.6), channel_id=1, replica_groups=mesh['query'=8,'item'=4] {'query'}, dimensions={0}, use_global_device_ids=true | all-gather | bytes 294912 | tf_op jit(solution)/shard_map/all_gather | solution.py:18
  82.7 0.3 broadcast_in_dim.19
  83.0 0.0 copy-start.3
  83.0 0.3 copy.30
  83.3 0.6 copy.21
  83.9 0.0 copy-done
  83.9 0.0 copy-done.2
  84.0 0.4 fusion.11
  84.4 0.0 copy-done.3
  84.4 0.0 copy-start.1
  84.4 0.4 convolution_convert_fusion
  84.8 0.5 copy-done.1
  85.4 8.0 %all_gather.20 = bf16[1024,256]{1,0:T(8,128)(2,1)S(1)} all-gather(bf16[256,256]{1,0:T(8,128)(2,1)S(1)} %convolution_convert_fusion), channel_id=1, replica_groups=mesh['query'=8,'item'=4] {'item'}, dimensions={0}, use_global_device_ids=true | all-gather | bytes 655360 | tf_op jit(solution)/shard_map/all_gather | solution.py:34
  93.4 0.6 fusion.3
  93.9 0.8 select_reduce_fusion
  94.8 30.5 %all-gather.2 = f32[8,3,512]{2,1,0:T(4,128)S(1)} all-gather(f32[1,3,512]{2,1,0:T(4,128)S(1)} %maximum_bitcast_fusion), channel_id=3, replica_groups=mesh['query'=8,'item'=4] {'query'}, dimensions={0}, use_global_device_ids=true | all-gather | bytes 55296 | tf_op jit(solution)/shard_map/all_gather | solution.py:48
  125.3 0.1 fusion.24
  125.4 0.8 fusion.2
  126.2 1.4 convolution_multiply_fusion.1
  127.6 0.0 reduce-scatter.5.cloned.1.call-update
  127.7 0.0 all-reduce.8.cloned.1.call-start
  127.7 23.9 %reduce-scatter.5.cloned.1.call-done = f32[256,256]{1,0:T(8,128)} async-done(((f32[1024,256]{1,0:T(8,128)}), f32[256,256]{1,0:T(8,128)}) %reduce-scatter.5.cloned.1.call-update) | async-done | bytes 262160 | tf_op jit(solution)/shard_map/reduce_scatter | solution.py:58
  151.6 2.8 fusion.13
  154.4 3.5 convolution_bitcast_fusion
  157.8 0.0 all-reduce.8.cloned.1.call-update
  157.8 0.0 all-reduce.6.cloned.1.call-start
  157.9 68.7 %all-reduce.8.cloned.1.call-done = (f32[512,1024]{0,1:T(8,128)}, f32[1024,256]{1,0:T(8,128)}) async-done(((f32[512,1024]{0,1:T(8,128)}, f32[1024,256]{1,0:T(8,128)}), (f32[512,1024]{0,1:T(8,128)}, f32[1024,256]{1,0:T(8,128)})) %all-reduce.8.cloned.1.call-update) | async-done | bytes 3145744 | tf_op jit(solution)/shard_map/psum | solution.py:68
  226.6 0.0 all-reduce.6.cloned.1.call-update
  226.7 0.0 reduce-scatter.3.cloned.1.call-start
  226.7 1.3 convolution_multiply_fusion.2
  228.0 0.0 reduce-scatter.3.cloned.1.call-update
  228.0 0.6 dynamic_slice.15
  228.6 131.7 %all-reduce.6.cloned.1.call-done = (f32[512,1024]{0,1:T(8,128)}, f32[1024,256]{1,0:T(8,128)}) async-done(((f32[512,1024]{0,1:T(8,128)}, f32[1024,256]{1,0:T(8,128)}), (f32[512,1024]{0,1:T(8,128)}, f32[1024,256]{1,0:T(8,128)})) %all-reduce.6.cloned.1.call-update) | async-done | bytes 3145744 | tf_op jit(solution)/shard_map/psum | solution.py:69
  360.3 1.8 broadcast_multiply_fusion
  362.1 1.8 copy.25
  364.0 2.3 broadcast_multiply_fusion.1
  366.2 58.7 %reduce-scatter.3.cloned.1.call-done = f32[64,256]{1,0:T(8,128)} async-done(((f32[512,256]{1,0:T(8,128)}), f32[64,256]{1,0:T(8,128)}) %reduce-scatter.3.cloned.1.call-update) | async-done | bytes 65552 | tf_op jit(solution)/shard_map/reduce_scatter | solution.py:62
  (8 shorter events, 0.1 us)
Async XLA Ops:
  7.2 76.8 %copy-start = (bf16[512,1024]{1,0:T(8,128)(2,1)S(1)}, bf16[512,1024]{1,0:T(8,128)(2,1)}, u32[]{:S(2)}) copy-start(bf16[512,1024]{1,0:T(8,128)(2,1)} %param.10) | copy-start | bytes 3145732
  7.2 76.8 %copy-start.2 = (bf16[1,256,512]{2,1,0:T(8,128)(2,1)S(1)}, bf16[1,256,512]{2,1,0:T(8,128)(2,1)}, u32[]{:S(2)}) copy-start(bf16[1,256,512]{2,1,0:T(8,128)(2,1)} %param.9) | copy-start | bytes 786436
  7.2 144.4 %reduce-scatter.5.cloned.1.call-start = ((), (), s32[]{:S(2)}) async-start(), calls=%async_computation.3 | async-start | bytes 1310720 | tf_op jit(solution)/shard_map/reduce_scatter | solution.py:58
  83.0 1.4 copy-start.3
  84.4 1.0 copy-start.1
  127.7 99.0 %all-reduce.8.cloned.1.call-start = ((), (), s32[]{:S(2)}) async-start(), calls=%async_computation.5 | async-start | bytes 6291456 | tf_op jit(solution)/shard_map/psum | solution.py:68
  157.8 202.4 %all-reduce.6.cloned.1.call-start = ((), (), s32[]{:S(2)}) async-start(), calls=%async_computation.4 | async-start | bytes 6291456 | tf_op jit(solution)/shard_map/psum | solution.py:69
  226.7 198.3 %reduce-scatter.3.cloned.1.call-start = ((), (), s32[]{:S(2)}) async-start(), calls=%async_computation.2 | async-start | bytes 589824 | tf_op jit(solution)/shard_map/reduce_scatter | solution.py:62
Sparse Core Ops, SparseCore 0:
  127.8 23.7 reduce-scatter.4
  158.0 68.6 all-reduce.7
  230.8 129.4 all-reduce.5
  364.1 60.8 reduce-scatter.2
